TPU v7x, 32 devices: a whole 2x2x4 slice. The times are simulated.
32 devices in a mesh: grp: 2 (over x), tile: 8 (over z, y), wave: 2 (over core).
Axes of the slice: x: 2, y: 2, z: 4, core: 2. Of those that a mesh axis runs over, the one named last changes fastest.
Arguments:
- residual: float32 [16, 8, 2, 8, 128], P(('grp', 'tile'), 'wave'), parts along dimension 0, may hold values from -210 to 210
- kernel: bfloat16 [16, 8, 9, 2, 128, 128], P(('grp', 'tile'), 'wave'), parts along dimension 0, may hold values from -0.125 to 0.125
- offsets: float32 [16, 8, 2, 128], P(('grp', 'tile'), 'wave'), parts along dimension 0, may hold values from 0 to 1
- neighbor: int32 [16, 8, 9], P(('grp', 'tile'), 'wave'), parts along dimension 0, may hold values from 0 to 8, each once within a row
- frequency: int32 [16], P('grp'), parts along dimension 0, may hold values from 0 to 7, each once
- lattice_x: int32 [128], replicated, may hold values from 0 to 127, each once
- lattice_y: int32 [128], replicated, may hold values from 0 to 127, each once
- spectral_weight: float32 [8, 128, 128], replicated, may hold values from 0.1 to 3
Outputs:
- image_two: float32 [16, 8, 2, 8, 128], P(('grp', 'tile'), 'wave'), parts along dimension 0
- arnoldi: float32 [8, 8], P('grp'), parts along dimension 0
There are 2 independent parts, one for each index of `grp`. A program takes and returns all parts, laid end to end along the dimension named above; an argument that names none is the same for every part. Nothing has to cross between parts.
Inputs may be any that keep to these rules, and one draw needn't show every extreme that they name: `neighbor`: each row names each of the nine neighbour slots once. `frequency`: each index appears once. `lattice_x`: each index appears once. `lattice_y`: each index appears once.
All inputs are finite; a program needn't handle non-finite values.
Results may differ from a plain program's by a relative error of at most 0.013.
Values may be sent and summed in bfloat16 or wider, within the bound.
A program may use at most 64 MiB of HBM per device.

v0:
```python
import math
import jax
import jax.numpy as jnp
from jax import lax
from jax.sharding import PartitionSpec as P

two_pi = 2.0 * math.pi
eps_norm = 1e-06


def padded_2(array, sides, width):
    for axis, dim in sides:
        size, length = (lax.axis_size(axis), array.shape[dim])
        up = [(i, (i + 1) % size) for i in range(size)]
        down = [(j, i) for i, j in up]
        last = lax.slice_in_dim(array, length - width, length, axis=dim)
        initial = lax.slice_in_dim(array, 0, width, axis=dim)
        before = lax.ppermute(last, axis, up)
        after = lax.ppermute(initial, axis, down)
        array = jnp.concatenate([before, array, after], axis=dim)
    return array


def phase_table(position, harmonic):
    phase_angle = two_pi * (position[:, None] * harmonic[None, :])
    return (jnp.cos(phase_angle).astype(jnp.bfloat16), jnp.sin(phase_angle).astype(jnp.bfloat16))


def project_rows(cosine_cols, sine_cols, twisted):
    row_count = cosine_cols.shape[1]
    stacked = jnp.concatenate([cosine_cols, sine_cols], 1)
    gram_matrix = lax.dot_general(
        stacked, twisted, (((0,), (0,)), ((), ())), preferred_element_type=jnp.float32
    )
    gram_matrix = gram_matrix.reshape(2, row_count, 2, -1)
    coef_real = gram_matrix[0, :, 0] + gram_matrix[1, :, 1]
    coef_imag = gram_matrix[0, :, 1] - gram_matrix[1, :, 0]
    return jnp.stack([coef_real, coef_imag], 1)


def expand_rows(cosine_cols, sine_cols, scaled):
    row_count = scaled.shape[0]
    upper_rows = scaled.reshape(row_count, -1)
    lower_rows = jnp.stack([-scaled[:, 1], scaled[:, 0]], 1).reshape(row_count, -1)
    matrix = jnp.concatenate([upper_rows, lower_rows], 0)
    stacked = jnp.concatenate([cosine_cols, sine_cols], 1)
    return jnp.dot(stacked, matrix, preferred_element_type=jnp.float32)


def twist_density(panel_density, cosine_y, sine_y):
    density_real = panel_density[:, 0, :, None].astype(jnp.float32)
    density_imag = panel_density[:, 1, :, None].astype(jnp.float32)
    wave_cos = cosine_y.astype(jnp.float32)[:, None, :]
    wave_sin = sine_y.astype(jnp.float32)[:, None, :]
    part_real = wave_cos * density_real + wave_sin * density_imag
    part_imag = wave_cos * density_imag - wave_sin * density_real
    return (
        jnp.stack([part_real, part_imag], 1)
        .reshape(panel_density.shape[0], -1)
        .astype(jnp.bfloat16)
    )


def finish(summed, cosine_y, sine_y, vectors):
    shaped = summed.reshape(summed.shape[0], 2, vectors, -1)
    wave_cos = cosine_y.astype(jnp.float32)[:, None, :]
    wave_sin = sine_y.astype(jnp.float32)[:, None, :]
    far_real = jnp.sum(shaped[:, 0] * wave_cos - shaped[:, 1] * wave_sin, -1)
    far_imag = jnp.sum(shaped[:, 0] * wave_sin + shaped[:, 1] * wave_cos, -1)
    return jnp.stack([far_real, far_imag], 1)


def combine_near(product, vectors):
    first_half = product[:, 0]
    second = product[:, 1]
    near_real = first_half[:, :vectors] - second[:, vectors:]
    near_imag = second[:, :vectors] + first_half[:, vectors:]
    return jnp.stack([near_real, near_imag], 1)


def panel_sum(values):
    return jnp.sum(values, axis=(0, 1, 3))


def per_device(
    residual, kernel, offsets, neighbor, frequency, lattice_x, lattice_y, spectral_weight
):
    strips = residual.shape[0]
    tiles_y = residual.shape[1]
    vectors = residual.shape[3]
    panels_t = residual.shape[4]
    modes_x = spectral_weight.shape[1]
    modes_y = spectral_weight.shape[2]
    count_x = lax.axis_size("tile") * strips
    count_y = lax.axis_size("wave") * tiles_y
    devices = lax.axis_size("tile") * lax.axis_size("wave")
    panels = count_x * count_y * panels_t
    local_rows = strips * tiles_y * panels_t
    column = (lax.axis_index("tile") * strips + jnp.arange(strips)).astype(jnp.float32)
    row_index = (lax.axis_index("wave") * tiles_y + jnp.arange(tiles_y)).astype(jnp.float32)
    position_x = ((column[:, None, None] + offsets[:, :, 0, :]) / count_x).reshape(-1)
    position_y = ((row_index[None, :, None] + offsets[:, :, 1, :]) / count_y).reshape(-1)
    harmonic_x = (lattice_x - modes_x // 2).astype(jnp.float32)
    harmonic_y = (lattice_y - modes_y // 2).astype(jnp.float32)
    cosine_x, sine_x = phase_table(position_x, harmonic_x)
    cosine_y, sine_y = phase_table(position_y, harmonic_y)
    weight_rows = jnp.take(spectral_weight, frequency, axis=0)
    factor = weight_rows * (1.0 / math.sqrt(modes_x * modes_y * panels))
    factor_wide = jnp.transpose(factor, (1, 0, 2)).reshape(modes_x, vectors * modes_y)[:, None, :]

    def near_field(density):
        padded = padded_2(density, (("tile", 0), ("wave", 1)), 1)
        candidates = []
        for slot_index in range(9):
            shift_x = slot_index // 3 - 1
            shift_y = slot_index % 3 - 1
            candidates.append(
                padded[1 + shift_x : 1 + shift_x + strips, 1 + shift_y : 1 + shift_y + tiles_y]
            )
        stacked = jnp.stack(candidates, 2).reshape(strips * tiles_y, 9, -1)
        picked = jnp.take_along_axis(stacked, neighbor.reshape(strips * tiles_y, 9, 1), axis=1)
        picked = picked.reshape(strips * tiles_y, 9, 2 * vectors, panels_t)
        blocks = kernel.reshape(strips * tiles_y, 9, 2, panels_t, panels_t)
        product = jnp.einsum("tjmp,tjcpq->tcmq", picked, blocks, preferred_element_type=jnp.float32)
        return combine_near(product, vectors).reshape(strips, tiles_y, 2, vectors, panels_t)

    def far_field(density):
        panel_density = jnp.transpose(density, (0, 1, 4, 2, 3)).reshape(local_rows, 2, vectors)
        twisted = twist_density(panel_density, cosine_y, sine_y)
        partial_coeffs = project_rows(cosine_x, sine_x, twisted)
        share_rows = modes_x // devices
        shares = lax.psum_scatter(partial_coeffs, ("tile", "wave"), scatter_dimension=0, tiled=True)
        owner_index = lax.axis_index("tile") * lax.axis_size("wave") + lax.axis_index("wave")
        owner_factor = lax.dynamic_slice_in_dim(
            factor_wide, owner_index * share_rows, share_rows, 0
        )
        owner_scaled = (shares * owner_factor).astype(jnp.bfloat16)
        scaled = lax.all_gather(owner_scaled, ("tile", "wave"), axis=0, tiled=True)
        summed = expand_rows(cosine_x, sine_x, scaled)
        far_panel = finish(summed, cosine_y, sine_y, vectors)
        return far_panel.reshape(strips, tiles_y, panels_t, 2, vectors).transpose(0, 1, 3, 4, 2)

    def apply_operator(density):
        return 0.5 * density.astype(jnp.float32) + near_field(density) + far_field(density)

    local_sq = panel_sum(
        residual[:, :, 0] * residual[:, :, 0] + residual[:, :, 1] * residual[:, :, 1]
    )
    squares = lax.psum(local_sq, ("tile", "wave"))
    basis_scale = jnp.sqrt(squares / panels + eps_norm)
    basis_one = (residual / basis_scale[None, None, None, :, None]).astype(jnp.bfloat16)
    image_one = apply_operator(basis_one)
    basis_real = basis_one[:, :, 0].astype(jnp.float32)
    basis_imag = basis_one[:, :, 1].astype(jnp.float32)
    image_real = image_one[:, :, 0]
    image_imag = image_one[:, :, 1]
    inner_real, inner_imag = lax.psum(
        (
            panel_sum(basis_real * image_real + basis_imag * image_imag),
            panel_sum(basis_real * image_imag - basis_imag * image_real),
        ),
        ("tile", "wave"),
    )
    coef_real = inner_real / panels
    coef_imag = inner_imag / panels
    wide_real = coef_real[None, None, :, None]
    wide_imag = coef_imag[None, None, :, None]
    update_real = image_real - (wide_real * basis_real - wide_imag * basis_imag)
    update_imag = image_imag - (wide_real * basis_imag + wide_imag * basis_real)
    update_sq = lax.psum(
        panel_sum(update_real * update_real + update_imag * update_imag), ("tile", "wave")
    )
    update_scale = jnp.sqrt(update_sq / panels + eps_norm)
    next_basis = (
        jnp.stack([update_real, update_imag], 2) / update_scale[None, None, None, :, None]
    ).astype(jnp.bfloat16)
    image_two = apply_operator(next_basis)
    arnoldi = jnp.stack([basis_scale, coef_real, coef_imag, update_scale])
    return (image_two, arnoldi)


def solution(mesh):
    return jax.shard_map(
        per_device,
        mesh=mesh,
        in_specs=(
            P(("grp", "tile"), "wave", None, None, None),
            P(("grp", "tile"), "wave", None, None, None, None),
            P(("grp", "tile"), "wave", None, None),
            P(("grp", "tile"), "wave", None),
            P("grp"),
            P(),
            P(),
            P(),
        ),
        out_specs=(P(("grp", "tile"), "wave", None, None, None), P("grp", None)),
        check_vma=False,
    )
```

profile of v0, /device:TPU:0, one launch (start us, length us, event | category | flops | bytes accessed | tf_op | source)
XLA Modules:
  0.0 307.0 jit_solution(9363511399105179548)
XLA Ops:
  8.2 34.9 %psum.28 = f32[8]{0:T(128)S(1)} all-reduce(f32[8]{0:T(128)S(1)} %add_reduce_fusion.2), channel_id=1, replica_groups=mesh['grp'=2,'tile'=8,'wave'=2] {'tile','wave'}, use_global_device_ids=true, to_apply=%region_1.2 | all-reduce | flops 8 | bytes 64 | tf_op jit(solution)/shard_map/psum | solution.py:149
  43.7 1.4 fusion.22
  45.2 4.7 %collective-permute-start.1 = (bf16[1,4,2,8,128]{4,3,1,2,0:T(8,128)(2,1)}, bf16[1,4,2,8,128]{4,3,1,2,0:T(8,128)(2,1)}, u32[]{:S(2)}, u32[]{:S(2)}) collective-permute-start(bf16[1,4,2,8,128]{4,3,1,2,0:T(8,128)(2,1)} %fusion.22), channel_id=1, source_target_pairs={{2,0},{4,2},{6,4},{8,6},{10,8},{12,10},{14,12},{0,14},{3,1},{5,3},... | collective-permute-start | bytes 49160 | tf_op jit(solution)/shard_map/ppermute | solution.py:19
  54.7 1.1 cosine_convert_fusion.1
  56.9 1.1 pad_maximum_fusion.2
  58.7 1.6 gather_fusion
  61.7 1.2 copy.121
  63.0 1.3 pad_maximum_fusion.31
  67.8 1.2 copy.122
  73.7 1.5 gather_fusion.1
  76.5 36.3 %reduce-scatter.3.cloned.1.call-done = f32[8,2,1024]{2,0,1:T(8,128)} async-done(((f32[128,2,1024]{2,0,1:T(8,128)}), f32[8,2,1024]{2,0,1:T(8,128)}) %reduce-scatter.3.cloned.1.call-update) | async-done | bytes 65552 | tf_op jit(solution)/shard_map/reduce_scatter | solution.py:132
  113.7 20.8 %all_gather.6 = bf16[128,2,1024]{2,0,1:T(8,128)(2,1)S(1)} all-gather(bf16[8,2,1024]{2,0,1:T(8,128)(2,1)S(1)} %multiply_convert_fusion.1), channel_id=1, replica_groups=mesh['grp'=2,'tile'=8,'wave'=2] {'tile','wave'}, dimensions={0}, use_global_device_ids=true | all-gather | bytes 557056 | tf_op jit(solution)/shard_map/all_gather | solution.py:138
  136.3 1.1 pad_maximum_fusion.4
  138.4 2.0 convolution_bitcast_fusion.1
  141.4 1.2 subtract_reduce_fusion.1
  145.2 29.8 %all-reduce = (f32[8]{0:T(128)S(1)}, f32[8]{0:T(128)S(1)}) all-reduce(f32[8]{0:T(128)S(1)} %get-tuple-element.16, f32[8]{0:T(128)S(1)} %get-tuple-element.15), channel_id=1, replica_groups=mesh['grp'=2,'tile'=8,'wave'=2] {'tile','wave'}, use_global_device_ids=true, to_apply=%region_8.10 | all-reduce | flops 16 | bytes 128 | tf_op jit(solution)/shard_map/psum | solution.py:157
  176.7 29.5 %psum.31 = f32[8]{0:T(128)S(1)} all-reduce(f32[8]{0:T(128)S(1)} %fusion.40), channel_id=1, replica_groups=mesh['grp'=2,'tile'=8,'wave'=2] {'tile','wave'}, use_global_device_ids=true, to_apply=%region_10.12 | all-reduce | flops 8 | bytes 64 | tf_op jit(solution)/shard_map/psum | solution.py:170
  206.4 4.7 %collective-permute-start.5 = (bf16[1,4,2,8,128]{4,3,1,2,0:T(8,128)(2,1)S(1)}, bf16[1,4,2,8,128]{4,3,1,2,0:T(8,128)(2,1)S(1)}, u32[]{:S(2)}, u32[]{:S(2)}) collective-permute-start(bf16[1,4,2,8,128]{4,3,1,2,0:T(8,128)(2,1)S(1)} %fusion.20), channel_id=1, source_target_pairs={{2,0},{4,2},{6,4},{8,6},{10,8},{12,10},{14,12},{0,14},{3,1},{5,3},... | collective-permute-start | bytes 49160 | tf_op jit(solution)/shard_map/ppermute | solution.py:19
  213.7 1.1 pad_maximum_fusion.3
  217.2 1.5 gather_fusion.2
  219.4 50.2 %reduce-scatter.5.cloned.1.call-done = f32[8,2,1024]{2,0,1:T(8,128)} async-done(((f32[128,2,1024]{2,0,1:T(8,128)}), f32[8,2,1024]{2,0,1:T(8,128)}) %reduce-scatter.5.cloned.1.call-update) | async-done | bytes 65552 | tf_op jit(solution)/shard_map/reduce_scatter | solution.py:132
  270.5 20.8 %all_gather.7 = bf16[128,2,1024]{2,0,1:T(8,128)(2,1)S(1)} all-gather(bf16[8,2,1024]{2,0,1:T(8,128)(2,1)S(1)} %multiply_convert_fusion), channel_id=1, replica_groups=mesh['grp'=2,'tile'=8,'wave'=2] {'tile','wave'}, dimensions={0}, use_global_device_ids=true | all-gather | bytes 557056 | tf_op jit(solution)/shard_map/all_gather | solution.py:138
  295.1 2.0 convolution_bitcast_fusion
  298.1 1.2 subtract_reduce_fusion
  (197 shorter events, 39.9 us)
Async XLA Ops:
  7.2 68.3 %copy-start = (bf16[1,4,9,2,128,128]{5,4,3,2,1,0:T(8,128)(2,1)S(1)}, bf16[1,4,9,2,128,128]{5,4,3,2,1,0:T(8,128)(2,1)}, u32[]{:S(2)}) copy-start(bf16[1,4,9,2,128,128]{5,4,3,2,1,0:T(8,128)(2,1)} %param.11) | copy-start | bytes 7077892
  7.2 105.6 %reduce-scatter.3.cloned.1.call-start = ((), (), s32[]{:S(2)}) async-start(), calls=%async_computation.2 | async-start | bytes 1114112 | tf_op jit(solution)/shard_map/reduce_scatter | solution.py:132
  43.7 7.0 %copy-start.19 = (f32[8]{0:T(128)}, f32[8]{0:T(128)S(1)}, u32[]{:S(2)}) copy-start(f32[8]{0:T(128)S(1)} %get-tuple-element.68) | copy-start | bytes 100
  45.2 17.8 %collective-permute-start = (bf16[1,4,2,8,128]{4,3,1,2,0:T(8,128)(2,1)}, bf16[1,4,2,8,128]{4,3,1,2,0:T(8,128)(2,1)}, u32[]{:S(2)}, u32[]{:S(2)}) collective-permute-start(bf16[1,4,2,8,128]{4,3,1,2,0:T(8,128)(2,1)} %fusion.22), channel_id=1, source_target_pairs={{0,2},{2,4},{4,6},{6,8},{8,10},{10,12},{12,14},{14,0},{1,3},{3,5},... | collective-permute-start | bytes 49160 | tf_op jit(solution)/shard_map/ppermute | solution.py:18
  45.2 17.8 %collective-permute-start.1 = (bf16[1,4,2,8,128]{4,3,1,2,0:T(8,128)(2,1)}, bf16[1,4,2,8,128]{4,3,1,2,0:T(8,128)(2,1)}, u32[]{:S(2)}, u32[]{:S(2)}) collective-permute-start(bf16[1,4,2,8,128]{4,3,1,2,0:T(8,128)(2,1)} %fusion.22), channel_id=1, source_target_pairs={{2,0},{4,2},{6,4},{8,6},{10,8},{12,10},{14,12},{0,14},{3,1},{5,3},... | collective-permute-start | bytes 49160 | tf_op jit(solution)/shard_map/ppermute | solution.py:19
  53.9 12.3 %copy-start.1 = (f32[512,128]{0,1:T(8,128)}, f32[512,128]{0,1:T(8,128)S(1)}, u32[]{:S(2)}) copy-start(f32[512,128]{0,1:T(8,128)S(1)} %get-tuple-element.64) | copy-start | bytes 786436
  58.0 211.7 %reduce-scatter.5.cloned.1.call-start = ((), (), s32[]{:S(2)}) async-start(), calls=%async_computation.3 | async-start | bytes 1114112 | tf_op jit(solution)/shard_map/reduce_scatter | solution.py:132
  64.3 7.5 %collective-permute-start.2 = (bf16[3,1,2,8,128]{4,3,1,2,0:T(8,128)(2,1)}, bf16[3,1,2,8,128]{4,3,1,2,0:T(8,128)(2,1)}, u32[]{:S(2)}, u32[]{:S(2)}) collective-permute-start(bf16[3,1,2,8,128]{4,3,1,2,0:T(8,128)(2,1)} %get-tuple-element.56), channel_id=1, source_target_pairs={{0,1},{1,0},{2,3},{3,2},{4,5},{5,4},{6,7},{7,6},{8,9},{9,8},{10,11... | collective-permute-start | bytes 36872 | tf_op jit(solution)/shard_map/ppermute | solution.py:18
  67.7 7.5 %copy-start.21 = (pred[4,9]{1,0:T(4,128)(4,1)S(1)}, pred[4,9]{1,0:T(4,128)(4,1)}, u32[]{:S(2)}) copy-start(pred[4,9]{1,0:T(4,128)(4,1)} %and_bitcast_fusion) | copy-start | bytes 112
  69.0 43.9 %copy-start.16 = (f32[8,1,1024]{2,0,1:T(8,128)}, f32[8,1,1024]{2,0,1:T(8,128)S(1)}, u32[]{:S(2)}) copy-start(f32[8,1,1024]{2,0,1:T(8,128)S(1)} %copy.122) | copy-start | bytes 98308
  70.5 2.1 collective-permute-start.3
  134.4 4.0 %copy-start.10 = (bf16[512,128]{0,1:T(8,128)(2,1)S(1)}, bf16[512,128]{0,1:T(8,128)(2,1)}, u32[]{:S(2)}) copy-start(bf16[512,128]{0,1:T(8,128)(2,1)} %copy-done.9) | copy-start | bytes 393220
  141.4 2.0 copy-start.20
  141.4 69.8 %copy-start.2 = (f32[512,128]{0,1:T(8,128)S(1)}, f32[512,128]{0,1:T(8,128)}, u32[]{:S(2)}) copy-start(f32[512,128]{0,1:T(8,128)} %copy-done.1) | copy-start | bytes 786436
  176.7 38.0 %copy-start.12 = (f32[1,4,1,8,128]{4,3,1,2,0:T(8,128)}, f32[1,4,1,8,128]{4,3,1,2,0:T(8,128)S(1)}, u32[]{:S(2)}) copy-start(f32[1,4,1,8,128]{4,3,1,2,0:T(8,128)S(1)} %get-tuple-element.51) | copy-start | bytes 49156
  176.7 38.0 %copy-start.14 = (f32[1,4,1,8,128]{4,3,1,2,0:T(8,128)}, f32[1,4,1,8,128]{4,3,1,2,0:T(8,128)S(1)}, u32[]{:S(2)}) copy-start(f32[1,4,1,8,128]{4,3,1,2,0:T(8,128)S(1)} %get-tuple-element.52) | copy-start | bytes 49156
  206.4 8.4 %collective-permute-start.4 = (bf16[1,4,2,8,128]{4,3,1,2,0:T(8,128)(2,1)S(1)}, bf16[1,4,2,8,128]{4,3,1,2,0:T(8,128)(2,1)S(1)}, u32[]{:S(2)}, u32[]{:S(2)}) collective-permute-start(bf16[1,4,2,8,128]{4,3,1,2,0:T(8,128)(2,1)S(1)} %fusion.20), channel_id=1, source_target_pairs={{0,2},{2,4},{4,6},{6,8},{8,10},{10,12},{12,14},{14,0},{1,3},{3,5},... | collective-permute-start | bytes 49160 | tf_op jit(solution)/shard_map/ppermute | solution.py:18
  206.4 8.4 %collective-permute-start.5 = (bf16[1,4,2,8,128]{4,3,1,2,0:T(8,128)(2,1)S(1)}, bf16[1,4,2,8,128]{4,3,1,2,0:T(8,128)(2,1)S(1)}, u32[]{:S(2)}, u32[]{:S(2)}) collective-permute-start(bf16[1,4,2,8,128]{4,3,1,2,0:T(8,128)(2,1)S(1)} %fusion.20), channel_id=1, source_target_pairs={{2,0},{4,2},{6,4},{8,6},{10,8},{12,10},{14,12},{0,14},{3,1},{5,3},... | collective-permute-start | bytes 49160 | tf_op jit(solution)/shard_map/ppermute | solution.py:19
  214.8 4.0 %copy-start.22 = (pred[4,9]{1,0:T(4,128)(4,1)S(1)}, pred[4,9]{1,0:T(4,128)(4,1)}, u32[]{:S(2)}) copy-start(pred[4,9]{1,0:T(4,128)(4,1)} %and_bitcast_fusion) | copy-start | bytes 112
  214.8 1.2 collective-permute-start.7
  215.5 1.3 collective-permute-start.6
  218.7 51.0 %copy-start.17 = (f32[8,1,1024]{2,0,1:T(8,128)S(1)}, f32[8,1,1024]{2,0,1:T(8,128)}, u32[]{:S(2)}) copy-start(f32[8,1,1024]{2,0,1:T(8,128)} %copy-done.16) | copy-start | bytes 98308
  291.3 3.8 %copy-start.11 = (bf16[512,128]{0,1:T(8,128)(2,1)S(1)}, bf16[512,128]{0,1:T(8,128)(2,1)}, u32[]{:S(2)}) copy-start(bf16[512,128]{0,1:T(8,128)(2,1)} %copy-done.9) | copy-start | bytes 393220
  298.0 1.4 copy-start.15
  (11 other events, 11.5 us)
Sparse Core Ops, SparseCore 0:
  58.1 54.6 reduce-scatter.2
  214.9 54.7 reduce-scatter.4
where the time goes:
time: 308 us; the launch traced here: 307 us
  blocking collectives  136 us (44%)
  waiting for transfers between devices  87.3 us (28%)
  other arithmetic  30 us (10%)
  local copies, waits for them, and re-layouts  22.2 us (7%)
  between operations  14.9 us (5%)
  starting transfers between devices  10.7 us (3%)
  matrix products  6.26 us (2%)
    reduce_scatter x2, waiting for transfers between devices, far_field(): lax.psum_scatter(partial_coeffs, ('tile', 'wave'), scatter_dimension=0, t...  86.5 us
    all_gather x2, blocking collectives, far_field(): scaled = lax.all_gather(owner_scaled, ('tile', 'wave'), axis=0, tiled=True)  41.5 us
    psum x1, blocking collectives, per_device(): squares = lax.psum(local_sq, ('tile', 'wave'))  34.9 us
    psum x1, blocking collectives, per_device(): lax.psum((panel_sum(basis_real * image_real + basis_imag * image_imag), p...  29.8 us
    psum x1, blocking collectives, per_device(): lax.psum(panel_sum(update_real * update_real + update_imag * update_imag)...  29.5 us
    ppermute x4, starting transfers between devices, padded_2(): after = lax.ppermute(initial, axis, down)  10.1 us
  transfers between devices with their start and end apart: 10, of which 3 were waited for; matrix products, arithmetic and copies ran while one was open for 10% of the time, Pallas kernels for 0%

commit v1 on v0

--- a/solution.py
+++ b/solution.py
@@ -125,6 +125,30 @@
         return combine_near(product, vectors).reshape(strips, tiles_y, 2, vectors, panels_t)
 
     def far_field(density):
+
+        def list_routes_all(m):
+            b_now = jax.lax.axis_size(("tile", "wave"))
+            lower = jax.lax.axis_index(("tile", "wave"))
+            y1, piece_now, placed = (b_now, lower, m.shape[0])
+            all_blocks = tuple((k * y1 if p == 0 else k for p, k in enumerate(m.shape)))
+            high = lax.dynamic_update_slice_in_dim(
+                jnp.zeros(all_blocks, m.dtype), m, piece_now * placed, axis=0
+            )
+            m_next = top = m
+            for dev_i in tuple(range(1, y1 // 2 + 1)):
+                res = tuple(((p, (p + 1) % y1) for p in range(y1)))
+                m_next = jax.lax.ppermute(m_next, axis_name=("tile", "wave"), perm=res)
+                high = lax.dynamic_update_slice_in_dim(
+                    high, m_next, (piece_now - dev_i) % y1 * placed, axis=0
+                )
+                if 2 * dev_i < y1:
+                    w2 = tuple(((p, (p - 1) % y1) for p in range(y1)))
+                    top = jax.lax.ppermute(top, axis_name=("tile", "wave"), perm=w2)
+                    high = lax.dynamic_update_slice_in_dim(
+                        high, top, (piece_now + dev_i) % y1 * placed, axis=0
+                    )
+            return high
+
         panel_density = jnp.transpose(density, (0, 1, 4, 2, 3)).reshape(local_rows, 2, vectors)
         twisted = twist_density(panel_density, cosine_y, sine_y)
         partial_coeffs = project_rows(cosine_x, sine_x, twisted)
@@ -135,7 +159,7 @@
             factor_wide, owner_index * share_rows, share_rows, 0
         )
         owner_scaled = (shares * owner_factor).astype(jnp.bfloat16)
-        scaled = lax.all_gather(owner_scaled, ("tile", "wave"), axis=0, tiled=True)
+        scaled = list_routes_all(owner_scaled)
         summed = expand_rows(cosine_x, sine_x, scaled)
         far_panel = finish(summed, cosine_y, sine_y, vectors)
         return far_panel.reshape(strips, tiles_y, panels_t, 2, vectors).transpose(0, 1, 3, 4, 2)

time: 308 us -> 582 us (1.89); the launches traced: 307 us -> 571 us
  local copies, waits for them, and re-layouts: 22.2 us -> 241 us
  starting transfers between devices: 10.7 us -> 73.3 us
  blocking collectives: 136 us -> 98.3 us
  waiting for transfers between devices: 87.3 us -> 108 us
    dynamic_update_slice x0 -> x32, local copies, waits for them, and re-layouts: none -> 185 us  [the longest x16 93.6 us: list_routes_all(): lax.dynamic_update_slice_in_dim(high, m_next, (piece_now - dev_i) % y1 *...]
    ppermute x0 -> x30, starting transfers between devices: none -> 62.6 us  [the longest x14 62.4 us: list_routes_all(): top = jax.lax.ppermute(top, axis_name=('tile', 'wave'), perm=w2)]
    all_gather x2 -> x0, blocking collectives: 41.5 us -> none  [far_field(): scaled = lax.all_gather(owner_scaled, ('tile', 'wave'), axis=0, tiled=True)]
    ppermute x0 -> x30, local copies, waits for them, and re-layouts: none -> 37.3 us  [the longest x16 21.6 us: list_routes_all(): m_next = jax.lax.ppermute(m_next, axis_name=('tile', 'wave'), perm=res)]
    ppermute x0 -> x30, waiting for transfers between devices: none -> 18.4 us  [the longest x16 12 us: list_routes_all(): m_next = jax.lax.ppermute(m_next, axis_name=('tile', 'wave'), perm=res)]
  transfers between devices with their start and end apart: 10 -> 40, of which waited for: 3 -> 24; matrix products, arithmetic and copies ran while one was open for 10% -> 43% of each run, Pallas kernels for 0% -> 0%
where the time goes in v1:
time: 582 us; the launch traced here: 571 us
  local copies, waits for them, and re-layouts  241 us (41%)
  waiting for transfers between devices  108 us (19%)
  blocking collectives  98.3 us (17%)
  starting transfers between devices  73.3 us (13%)
  other arithmetic  32.1 us (6%)
  between operations  15.4 us (3%)
    dynamic_update_slice x16, local copies, waits for them, and re-layouts, list_routes_all(): lax.dynamic_update_slice_in_dim(high, m_next, (piece_now - dev_i) % y1 *...  93.6 us
    reduce_scatter x2, waiting for transfers between devices, far_field(): lax.psum_scatter(partial_coeffs, ('tile', 'wave'), scatter_dimension=0, t...  88.3 us
    dynamic_update_slice x14, local copies, waits for them, and re-layouts, list_routes_all(): lax.dynamic_update_slice_in_dim(high, top, (piece_now + dev_i) % y1 * pla...  81.6 us
    ppermute x14, starting transfers between devices, list_routes_all(): top = jax.lax.ppermute(top, axis_name=('tile', 'wave'), perm=w2)  62.4 us
    psum x1, blocking collectives, per_device(): squares = lax.psum(local_sq, ('tile', 'wave'))  34.9 us
    psum x1, blocking collectives, per_device(): lax.psum((panel_sum(basis_real * image_real + basis_imag * image_imag), p...  33.9 us
    psum x1, blocking collectives, per_device(): lax.psum(panel_sum(update_real * update_real + update_imag * update_imag)...  29.5 us
    ppermute x16, local copies, waits for them, and re-layouts, list_routes_all(): m_next = jax.lax.ppermute(m_next, axis_name=('tile', 'wave'), perm=res)  21.6 us
  transfers between devices with their start and end apart: 40, of which 24 were waited for; matrix products, arithmetic and copies ran while one was open for 43% of the time, Pallas kernels for 0%

profile of v1, /device:TPU:0, one launch (start us, length us, event | category | flops | bytes accessed | tf_op | source)
XLA Modules:
  0.0 571.5 jit_solution(10209974635053442312)
XLA Ops:
  8.2 34.9 %psum.28 = f32[8]{0:T(128)S(1)} all-reduce(f32[8]{0:T(128)S(1)} %add_reduce_fusion.2), channel_id=1, replica_groups=mesh['grp'=2,'tile'=8,'wave'=2] {'tile','wave'}, use_global_device_ids=true, to_apply=%region_1.2 | all-reduce | flops 8 | bytes 64 | tf_op jit(solution)/shard_map/psum | solution.py:173
  76.4 35.9 %reduce-scatter.3.cloned.1.call-done = f32[8,2,1024]{2,0,1:T(8,128)} async-done(((f32[128,2,1024]{2,0,1:T(8,128)}), f32[8,2,1024]{2,0,1:T(8,128)}) %reduce-scatter.3.cloned.1.call-update) | async-done | bytes 65552 | tf_op jit(solution)/shard_map/reduce_scatter | solution.py:156
  164.3 5.8 %dynamic_update_slice.97 = bf16[128,2,1024]{0,2,1:T(8,128)(2,1)S(1)} dynamic-update-slice(bf16[128,2,1024]{0,2,1:T(8,128)(2,1)S(1)} %dynamic_update_slice.96, bf16[8,2,1024]{0,2,1:T(8,128)(2,1)} %copy.180, s32[]{:T(128)S(6)} %select_n.180, s32[]{:T(128)} %constant.169.clone.1, s32[]{:T(128)} %constant.169.clone.1) | dynamic-update-slice | bytes 65540 | tf_op jit(solution)/shard_map/dynamic_update_slice | solution.py:141
  171.2 5.8 %dynamic_update_slice.98 = bf16[128,2,1024]{0,2,1:T(8,128)(2,1)S(1)} dynamic-update-slice(bf16[128,2,1024]{0,2,1:T(8,128)(2,1)S(1)} %dynamic_update_slice.97, bf16[8,2,1024]{0,2,1:T(8,128)(2,1)} %copy.181, s32[]{:T(128)S(6)} %select_n.182, s32[]{:T(128)} %constant.169.clone.1, s32[]{:T(128)} %constant.169.clone.1) | dynamic-update-slice | bytes 65540 | tf_op jit(solution)/shard_map/dynamic_update_slice | solution.py:147
  178.0 5.8 %dynamic_update_slice.99 = bf16[128,2,1024]{0,2,1:T(8,128)(2,1)S(1)} dynamic-update-slice(bf16[128,2,1024]{0,2,1:T(8,128)(2,1)S(1)} %dynamic_update_slice.98, bf16[8,2,1024]{0,2,1:T(8,128)(2,1)} %copy.182, s32[]{:T(128)S(6)} %select_n.184, s32[]{:T(128)} %constant.169.clone.1, s32[]{:T(128)} %constant.169.clone.1) | dynamic-update-slice | bytes 65540 | tf_op jit(solution)/shard_map/dynamic_update_slice | solution.py:141
  184.9 5.8 %dynamic_update_slice.100 = bf16[128,2,1024]{0,2,1:T(8,128)(2,1)S(1)} dynamic-update-slice(bf16[128,2,1024]{0,2,1:T(8,128)(2,1)S(1)} %dynamic_update_slice.99, bf16[8,2,1024]{0,2,1:T(8,128)(2,1)} %copy.183, s32[]{:T(128)S(6)} %select_n.186, s32[]{:T(128)} %constant.169.clone.1, s32[]{:T(128)} %constant.169.clone.1) | dynamic-update-slice | bytes 65540 | tf_op jit(solution)/shard_map/dynamic_update_slice | solution.py:147
  192.5 5.8 %dynamic_update_slice.101 = bf16[128,2,1024]{0,2,1:T(8,128)(2,1)S(1)} dynamic-update-slice(bf16[128,2,1024]{0,2,1:T(8,128)(2,1)S(1)} %dynamic_update_slice.100, bf16[8,2,1024]{0,2,1:T(8,128)(2,1)} %copy.184, s32[]{:T(128)S(6)} %select_n.188, s32[]{:T(128)} %constant.169.clone.1, s32[]{:T(128)} %constant.169.clone.1) | dynamic-update-slice | bytes 65540 | tf_op jit(solution)/shard_map/dynamic_update_slice | solution.py:141
  199.3 5.8 %dynamic_update_slice.102 = bf16[128,2,1024]{0,2,1:T(8,128)(2,1)S(1)} dynamic-update-slice(bf16[128,2,1024]{0,2,1:T(8,128)(2,1)S(1)} %dynamic_update_slice.101, bf16[8,2,1024]{0,2,1:T(8,128)(2,1)} %copy.185, s32[]{:T(128)S(6)} %select_n.190, s32[]{:T(128)} %constant.169.clone.1, s32[]{:T(128)} %constant.169.clone.1) | dynamic-update-slice | bytes 65540 | tf_op jit(solution)/shard_map/dynamic_update_slice | solution.py:147
  207.0 5.8 %dynamic_update_slice.103 = bf16[128,2,1024]{0,2,1:T(8,128)(2,1)S(1)} dynamic-update-slice(bf16[128,2,1024]{0,2,1:T(8,128)(2,1)S(1)} %dynamic_update_slice.102, bf16[8,2,1024]{0,2,1:T(8,128)(2,1)} %copy.186, s32[]{:T(128)S(6)} %select_n.192, s32[]{:T(128)} %constant.169.clone.1, s32[]{:T(128)} %constant.169.clone.1) | dynamic-update-slice | bytes 65540 | tf_op jit(solution)/shard_map/dynamic_update_slice | solution.py:141
  214.6 5.8 %dynamic_update_slice.104 = bf16[128,2,1024]{0,2,1:T(8,128)(2,1)S(1)} dynamic-update-slice(bf16[128,2,1024]{0,2,1:T(8,128)(2,1)S(1)} %dynamic_update_slice.103, bf16[8,2,1024]{0,2,1:T(8,128)(2,1)} %copy.187, s32[]{:T(128)S(6)} %select_n.194, s32[]{:T(128)} %constant.169.clone.1, s32[]{:T(128)} %constant.169.clone.1) | dynamic-update-slice | bytes 65540 | tf_op jit(solution)/shard_map/dynamic_update_slice | solution.py:147
  222.2 5.8 %dynamic_update_slice.105 = bf16[128,2,1024]{0,2,1:T(8,128)(2,1)S(1)} dynamic-update-slice(bf16[128,2,1024]{0,2,1:T(8,128)(2,1)S(1)} %dynamic_update_slice.104, bf16[8,2,1024]{0,2,1:T(8,128)(2,1)} %copy.188, s32[]{:T(128)S(6)} %select_n.196, s32[]{:T(128)} %constant.169.clone.1, s32[]{:T(128)} %constant.169.clone.1) | dynamic-update-slice | bytes 65540 | tf_op jit(solution)/shard_map/dynamic_update_slice | solution.py:141
  229.0 5.8 %dynamic_update_slice.106 = bf16[128,2,1024]{0,2,1:T(8,128)(2,1)S(1)} dynamic-update-slice(bf16[128,2,1024]{0,2,1:T(8,128)(2,1)S(1)} %dynamic_update_slice.105, bf16[8,2,1024]{0,2,1:T(8,128)(2,1)} %copy.189, s32[]{:T(128)S(6)} %select_n.198, s32[]{:T(128)} %constant.169.clone.1, s32[]{:T(128)} %constant.169.clone.1) | dynamic-update-slice | bytes 65540 | tf_op jit(solution)/shard_map/dynamic_update_slice | solution.py:147
  235.9 5.8 %dynamic_update_slice.107 = bf16[128,2,1024]{0,2,1:T(8,128)(2,1)S(1)} dynamic-update-slice(bf16[128,2,1024]{0,2,1:T(8,128)(2,1)S(1)} %dynamic_update_slice.106, bf16[8,2,1024]{0,2,1:T(8,128)(2,1)} %copy.190, s32[]{:T(128)S(6)} %select_n.200, s32[]{:T(128)} %constant.169.clone.1, s32[]{:T(128)} %constant.169.clone.1) | dynamic-update-slice | bytes 65540 | tf_op jit(solution)/shard_map/dynamic_update_slice | solution.py:141
  242.7 5.8 %dynamic_update_slice.108 = bf16[128,2,1024]{0,2,1:T(8,128)(2,1)S(1)} dynamic-update-slice(bf16[128,2,1024]{0,2,1:T(8,128)(2,1)S(1)} %dynamic_update_slice.107, bf16[8,2,1024]{0,2,1:T(8,128)(2,1)} %copy.191, s32[]{:T(128)S(6)} %select_n.202, s32[]{:T(128)} %constant.169.clone.1, s32[]{:T(128)} %constant.169.clone.1) | dynamic-update-slice | bytes 65540 | tf_op jit(solution)/shard_map/dynamic_update_slice | solution.py:147
  250.3 6.0 %dynamic_update_slice.109 = bf16[128,2,1024]{0,2,1:T(8,128)(2,1)S(1)} dynamic-update-slice(bf16[128,2,1024]{0,2,1:T(8,128)(2,1)S(1)} %dynamic_update_slice.108, bf16[8,2,1024]{0,2,1:T(8,128)(2,1)} %copy.192, s32[]{:T(128)S(6)} %select_n.204, s32[]{:T(128)} %constant.169.clone.1, s32[]{:T(128)} %constant.169.clone.1) | dynamic-update-slice | bytes 65540 | tf_op jit(solution)/shard_map/dynamic_update_slice | solution.py:141
  258.2 5.8 %dynamic_update_slice.110 = bf16[128,2,1024]{0,2,1:T(8,128)(2,1)S(1)} dynamic-update-slice(bf16[128,2,1024]{0,2,1:T(8,128)(2,1)S(1)} %dynamic_update_slice.109, bf16[8,2,1024]{0,2,1:T(8,128)(2,1)} %copy.193, s32[]{:T(128)S(6)} %select_n.206, s32[]{:T(128)} %constant.169.clone.1, s32[]{:T(128)} %constant.169.clone.1) | dynamic-update-slice | bytes 65540 | tf_op jit(solution)/shard_map/dynamic_update_slice | solution.py:147
  265.8 5.8 %dynamic_update_slice.111 = bf16[128,2,1024]{0,2,1:T(8,128)(2,1)S(1)} dynamic-update-slice(bf16[128,2,1024]{0,2,1:T(8,128)(2,1)S(1)} %dynamic_update_slice.110, bf16[8,2,1024]{0,2,1:T(8,128)(2,1)} %copy.194, s32[]{:T(128)S(6)} %select_n.208, s32[]{:T(128)} %constant.169.clone.1, s32[]{:T(128)} %constant.169.clone.1) | dynamic-update-slice | bytes 65540 | tf_op jit(solution)/shard_map/dynamic_update_slice | solution.py:141
  277.4 33.9 %all-reduce = (f32[8]{0:T(128)S(1)}, f32[8]{0:T(128)S(1)}) all-reduce(f32[8]{0:T(128)S(1)} %get-tuple-element.16, f32[8]{0:T(128)S(1)} %get-tuple-element.15), channel_id=1, replica_groups=mesh['grp'=2,'tile'=8,'wave'=2] {'tile','wave'}, use_global_device_ids=true, to_apply=%region_8.10 | all-reduce | flops 16 | bytes 128 | tf_op jit(solution)/shard_map/psum | solution.py:181
  313.0 29.5 %psum.31 = f32[8]{0:T(128)S(1)} all-reduce(f32[8]{0:T(128)S(1)} %fusion.40), channel_id=1, replica_groups=mesh['grp'=2,'tile'=8,'wave'=2] {'tile','wave'}, use_global_device_ids=true, to_apply=%region_10.12 | all-reduce | flops 8 | bytes 64 | tf_op jit(solution)/shard_map/psum | solution.py:194
  353.4 52.4 %reduce-scatter.5.cloned.1.call-done = f32[8,2,1024]{2,0,1:T(8,128)} async-done(((f32[128,2,1024]{2,0,1:T(8,128)}), f32[8,2,1024]{2,0,1:T(8,128)}) %reduce-scatter.5.cloned.1.call-update) | async-done | bytes 65552 | tf_op jit(solution)/shard_map/reduce_scatter | solution.py:156
  456.7 5.8 %dynamic_update_slice.113 = bf16[128,2,1024]{0,2,1:T(8,128)(2,1)S(1)} dynamic-update-slice(bf16[128,2,1024]{0,2,1:T(8,128)(2,1)S(1)} %dynamic_update_slice.112, bf16[8,2,1024]{0,2,1:T(8,128)(2,1)} %copy.218, s32[]{:T(128)S(6)} %select_n.180, s32[]{:T(128)} %constant.169.clone.1, s32[]{:T(128)} %constant.169.clone.1) | dynamic-update-slice | bytes 65540 | tf_op jit(solution)/shard_map/dynamic_update_slice | solution.py:141
  512.3 5.8 %dynamic_update_slice.121 = bf16[128,2,1024]{0,2,1:T(8,128)(2,1)S(1)} dynamic-update-slice(bf16[128,2,1024]{0,2,1:T(8,128)(2,1)S(1)} %dynamic_update_slice.120, bf16[8,2,1024]{0,2,1:T(8,128)(2,1)} %copy.226, s32[]{:T(128)S(6)} %select_n.196, s32[]{:T(128)} %constant.169.clone.1, s32[]{:T(128)} %constant.169.clone.1) | dynamic-update-slice | bytes 65540 | tf_op jit(solution)/shard_map/dynamic_update_slice | solution.py:141
  539.7 6.0 %dynamic_update_slice.125 = bf16[128,2,1024]{0,2,1:T(8,128)(2,1)S(1)} dynamic-update-slice(bf16[128,2,1024]{0,2,1:T(8,128)(2,1)S(1)} %dynamic_update_slice.124, bf16[8,2,1024]{0,2,1:T(8,128)(2,1)} %copy.230, s32[]{:T(128)S(6)} %select_n.204, s32[]{:T(128)} %constant.169.clone.1, s32[]{:T(128)} %constant.169.clone.1) | dynamic-update-slice | bytes 65540 | tf_op jit(solution)/shard_map/dynamic_update_slice | solution.py:141
  554.4 5.8 %dynamic_update_slice.127 = bf16[128,2,1024]{0,2,1:T(8,128)(2,1)S(1)} dynamic-update-slice(bf16[128,2,1024]{0,2,1:T(8,128)(2,1)S(1)} %dynamic_update_slice.126, bf16[8,2,1024]{0,2,1:T(8,128)(2,1)} %copy.232, s32[]{:T(128)S(6)} %select_n.208, s32[]{:T(128)} %constant.169.clone.1, s32[]{:T(128)} %constant.169.clone.1) | dynamic-update-slice | bytes 65540 | tf_op jit(solution)/shard_map/dynamic_update_slice | solution.py:141
  (323 shorter events, 258.3 us)
Async XLA Ops:
  7.2 105.1 %reduce-scatter.3.cloned.1.call-start = ((), (), s32[]{:S(2)}) async-start(), calls=%async_computation.2 | async-start | bytes 1114112 | tf_op jit(solution)/shard_map/reduce_scatter | solution.py:156
  44.6 24.0 %collective-permute-start = (bf16[1,4,2,8,128]{4,3,1,2,0:T(8,128)(2,1)S(1)}, bf16[1,4,2,8,128]{4,3,1,2,0:T(8,128)(2,1)}, u32[]{:S(2)}, u32[]{:S(2)}) collective-permute-start(bf16[1,4,2,8,128]{4,3,1,2,0:T(8,128)(2,1)S(1)} %fusion.22), channel_id=1, source_target_pairs={{0,2},{2,4},{4,6},{6,8},{8,10},{10,12},{12,14},{14,0},{1,3},{3,5},... | collective-permute-start | bytes 49160 | tf_op jit(solution)/shard_map/ppermute | solution.py:18
  44.6 24.0 %collective-permute-start.1 = (bf16[1,4,2,8,128]{4,3,1,2,0:T(8,128)(2,1)S(1)}, bf16[1,4,2,8,128]{4,3,1,2,0:T(8,128)(2,1)}, u32[]{:S(2)}, u32[]{:S(2)}) collective-permute-start(bf16[1,4,2,8,128]{4,3,1,2,0:T(8,128)(2,1)S(1)} %fusion.22), channel_id=1, source_target_pairs={{2,0},{4,2},{6,4},{8,6},{10,8},{12,10},{14,12},{0,14},{3,1},{5,3},... | collective-permute-start | bytes 49160 | tf_op jit(solution)/shard_map/ppermute | solution.py:19
  57.4 348.4 %reduce-scatter.5.cloned.1.call-start = ((), (), s32[]{:S(2)}) async-start(), calls=%async_computation.3 | async-start | bytes 1114112 | tf_op jit(solution)/shard_map/reduce_scatter | solution.py:156
  119.2 6.1 %collective-permute-start.6 = (bf16[8,2,1024]{2,0,1:T(8,128)(2,1)S(1)}, bf16[8,2,1024]{2,0,1:T(8,128)(2,1)S(1)}, u32[]{:S(2)}, u32[]{:S(2)}) collective-permute-start(bf16[8,2,1024]{2,0,1:T(8,128)(2,1)S(1)} %collective-permute-done.4), channel_id=1, source_target_pairs={{0,1},{1,2},{2,3},{3,4},{4,5},{5,6},{6,7},{7,8},{8,9},{9,10},{10,1... | collective-permute-start | bytes 98312 | tf_op jit(solution)/shard_map/ppermute | solution.py:140
  119.3 6.1 %collective-permute-start.7 = (bf16[8,2,1024]{2,0,1:T(8,128)(2,1)S(1)}, bf16[8,2,1024]{2,0,1:T(8,128)(2,1)S(1)}, u32[]{:S(2)}, u32[]{:S(2)}) collective-permute-start(bf16[8,2,1024]{2,0,1:T(8,128)(2,1)S(1)} %collective-permute-done.5), channel_id=1, source_target_pairs={{0,15},{1,0},{2,1},{3,2},{4,3},{5,4},{6,5},{7,6},{8,7},{9,8},{10,9... | collective-permute-start | bytes 98312 | tf_op jit(solution)/shard_map/ppermute | solution.py:146
  125.3 6.1 %collective-permute-start.8 = (bf16[8,2,1024]{2,0,1:T(8,128)(2,1)S(1)}, bf16[8,2,1024]{2,0,1:T(8,128)(2,1)}, u32[]{:S(2)}, u32[]{:S(2)}) collective-permute-start(bf16[8,2,1024]{2,0,1:T(8,128)(2,1)S(1)} %collective-permute-done.6), channel_id=1, source_target_pairs={{0,1},{1,2},{2,3},{3,4},{4,5},{5,6},{6,7},{7,8},{8,9},{9,10},{10,1... | collective-permute-start | bytes 98312 | tf_op jit(solution)/shard_map/ppermute | solution.py:140
  125.4 7.7 %collective-permute-start.9 = (bf16[8,2,1024]{2,0,1:T(8,128)(2,1)S(1)}, bf16[8,2,1024]{2,0,1:T(8,128)(2,1)S(1)}, u32[]{:S(2)}, u32[]{:S(2)}) collective-permute-start(bf16[8,2,1024]{2,0,1:T(8,128)(2,1)S(1)} %collective-permute-done.7), channel_id=1, source_target_pairs={{0,15},{1,0},{2,1},{3,2},{4,3},{5,4},{6,5},{7,6},{8,7},{9,8},{10,9... | collective-permute-start | bytes 98312 | tf_op jit(solution)/shard_map/ppermute | solution.py:146
  131.5 6.4 %collective-permute-start.10 = (bf16[8,2,1024]{2,0,1:T(8,128)(2,1)}, bf16[8,2,1024]{2,0,1:T(8,128)(2,1)}, u32[]{:S(2)}, u32[]{:S(2)}) collective-permute-start(bf16[8,2,1024]{2,0,1:T(8,128)(2,1)} %collective-permute-done.8), channel_id=1, source_target_pairs={{0,1},{1,2},{2,3},{3,4},{4,5},{5,6},{6,7},{7,8},{8,9},{9,10},{10,1... | collective-permute-start | bytes 98312 | tf_op jit(solution)/shard_map/ppermute | solution.py:140
  137.8 6.4 %collective-permute-start.12 = (bf16[8,2,1024]{2,0,1:T(8,128)(2,1)}, bf16[8,2,1024]{2,0,1:T(8,128)(2,1)}, u32[]{:S(2)}, u32[]{:S(2)}) collective-permute-start(bf16[8,2,1024]{2,0,1:T(8,128)(2,1)} %collective-permute-done.10), channel_id=1, source_target_pairs={{0,1},{1,2},{2,3},{3,4},{4,5},{5,6},{6,7},{7,8},{8,9},{9,10},{10,1... | collective-permute-start | bytes 98312 | tf_op jit(solution)/shard_map/ppermute | solution.py:140
  139.2 6.5 %collective-permute-start.13 = (bf16[8,2,1024]{2,0,1:T(8,128)(2,1)}, bf16[8,2,1024]{2,0,1:T(8,128)(2,1)S(1)}, u32[]{:S(2)}, u32[]{:S(2)}) collective-permute-start(bf16[8,2,1024]{2,0,1:T(8,128)(2,1)} %collective-permute-done.11), channel_id=1, source_target_pairs={{0,15},{1,0},{2,1},{3,2},{4,3},{5,4},{6,5},{7,6},{8,7},{9,8},{10,9... | collective-permute-start | bytes 98312 | tf_op jit(solution)/shard_map/ppermute | solution.py:146
  144.2 6.3 %collective-permute-start.14 = (bf16[8,2,1024]{2,0,1:T(8,128)(2,1)}, bf16[8,2,1024]{2,0,1:T(8,128)(2,1)S(1)}, u32[]{:S(2)}, u32[]{:S(2)}) collective-permute-start(bf16[8,2,1024]{2,0,1:T(8,128)(2,1)} %collective-permute-done.12), channel_id=1, source_target_pairs={{0,1},{1,2},{2,3},{3,4},{4,5},{5,6},{6,7},{7,8},{8,9},{9,10},{10,1... | collective-permute-start | bytes 98312 | tf_op jit(solution)/shard_map/ppermute | solution.py:140
  150.5 6.1 %collective-permute-start.16 = (bf16[8,2,1024]{2,0,1:T(8,128)(2,1)S(1)}, bf16[8,2,1024]{2,0,1:T(8,128)(2,1)}, u32[]{:S(2)}, u32[]{:S(2)}) collective-permute-start(bf16[8,2,1024]{2,0,1:T(8,128)(2,1)S(1)} %collective-permute-done.14), channel_id=1, source_target_pairs={{0,1},{1,2},{2,3},{3,4},{4,5},{5,6},{6,7},{7,8},{8,9},{9,10},{10,1... | collective-permute-start | bytes 98312 | tf_op jit(solution)/shard_map/ppermute | solution.py:140
  151.6 104.8 %collective-permute-start.17 = (bf16[8,2,1024]{2,0,1:T(8,128)(2,1)S(1)}, bf16[8,2,1024]{2,0,1:T(8,128)(2,1)}, u32[]{:S(2)}, u32[]{:S(2)}) collective-permute-start(bf16[8,2,1024]{2,0,1:T(8,128)(2,1)S(1)} %collective-permute-done.15), channel_id=1, source_target_pairs={{0,15},{1,0},{2,1},{3,2},{4,3},{5,4},{6,5},{7,6},{8,7},{9,8},{10,9... | collective-permute-start | bytes 98312 | tf_op jit(solution)/shard_map/ppermute | solution.py:146
  156.6 107.4 %collective-permute-start.18 = (bf16[8,2,1024]{2,0,1:T(8,128)(2,1)}, bf16[8,2,1024]{2,0,1:T(8,128)(2,1)}, u32[]{:S(2)}, u32[]{:S(2)}) collective-permute-start(bf16[8,2,1024]{2,0,1:T(8,128)(2,1)} %collective-permute-done.16), channel_id=1, source_target_pairs={{0,1},{1,2},{2,3},{3,4},{4,5},{5,6},{6,7},{7,8},{8,9},{9,10},{10,1... | collective-permute-start | bytes 98312 | tf_op jit(solution)/shard_map/ppermute | solution.py:140
  342.7 8.4 %collective-permute-start.19 = (bf16[1,4,2,8,128]{4,3,1,2,0:T(8,128)(2,1)S(1)}, bf16[1,4,2,8,128]{4,3,1,2,0:T(8,128)(2,1)S(1)}, u32[]{:S(2)}, u32[]{:S(2)}) collective-permute-start(bf16[1,4,2,8,128]{4,3,1,2,0:T(8,128)(2,1)S(1)} %fusion.20), channel_id=1, source_target_pairs={{0,2},{2,4},{4,6},{6,8},{8,10},{10,12},{12,14},{14,0},{1,3},{3,5},... | collective-permute-start | bytes 49160 | tf_op jit(solution)/shard_map/ppermute | solution.py:18
  342.7 8.4 %collective-permute-start.20 = (bf16[1,4,2,8,128]{4,3,1,2,0:T(8,128)(2,1)S(1)}, bf16[1,4,2,8,128]{4,3,1,2,0:T(8,128)(2,1)S(1)}, u32[]{:S(2)}, u32[]{:S(2)}) collective-permute-start(bf16[1,4,2,8,128]{4,3,1,2,0:T(8,128)(2,1)S(1)} %fusion.20), channel_id=1, source_target_pairs={{2,0},{4,2},{6,4},{8,6},{10,8},{12,10},{14,12},{0,14},{3,1},{5,3},... | collective-permute-start | bytes 49160 | tf_op jit(solution)/shard_map/ppermute | solution.py:19
  412.7 6.1 %collective-permute-start.25 = (bf16[8,2,1024]{2,0,1:T(8,128)(2,1)S(1)}, bf16[8,2,1024]{2,0,1:T(8,128)(2,1)S(1)}, u32[]{:S(2)}, u32[]{:S(2)}) collective-permute-start(bf16[8,2,1024]{2,0,1:T(8,128)(2,1)S(1)} %collective-permute-done.23), channel_id=1, source_target_pairs={{0,1},{1,2},{2,3},{3,4},{4,5},{5,6},{6,7},{7,8},{8,9},{9,10},{10,1... | collective-permute-start | bytes 98312 | tf_op jit(solution)/shard_map/ppermute | solution.py:140
  412.8 6.1 %collective-permute-start.26 = (bf16[8,2,1024]{2,0,1:T(8,128)(2,1)S(1)}, bf16[8,2,1024]{2,0,1:T(8,128)(2,1)S(1)}, u32[]{:S(2)}, u32[]{:S(2)}) collective-permute-start(bf16[8,2,1024]{2,0,1:T(8,128)(2,1)S(1)} %collective-permute-done.24), channel_id=1, source_target_pairs={{0,15},{1,0},{2,1},{3,2},{4,3},{5,4},{6,5},{7,6},{8,7},{9,8},{10,9... | collective-permute-start | bytes 98312 | tf_op jit(solution)/shard_map/ppermute | solution.py:146
  418.9 7.6 %collective-permute-start.28 = (bf16[8,2,1024]{2,0,1:T(8,128)(2,1)S(1)}, bf16[8,2,1024]{2,0,1:T(8,128)(2,1)S(1)}, u32[]{:S(2)}, u32[]{:S(2)}) collective-permute-start(bf16[8,2,1024]{2,0,1:T(8,128)(2,1)S(1)} %collective-permute-done.26), channel_id=1, source_target_pairs={{0,15},{1,0},{2,1},{3,2},{4,3},{5,4},{6,5},{7,6},{8,7},{9,8},{10,9... | collective-permute-start | bytes 98312 | tf_op jit(solution)/shard_map/ppermute | solution.py:146
  430.9 6.1 %collective-permute-start.31 = (bf16[8,2,1024]{2,0,1:T(8,128)(2,1)S(1)}, bf16[8,2,1024]{2,0,1:T(8,128)(2,1)}, u32[]{:S(2)}, u32[]{:S(2)}) collective-permute-start(bf16[8,2,1024]{2,0,1:T(8,128)(2,1)S(1)} %collective-permute-done.29), channel_id=1, source_target_pairs={{0,1},{1,2},{2,3},{3,4},{4,5},{5,6},{6,7},{7,8},{8,9},{9,10},{10,1... | collective-permute-start | bytes 98312 | tf_op jit(solution)/shard_map/ppermute | solution.py:140
  437.1 6.3 %collective-permute-start.33 = (bf16[8,2,1024]{2,0,1:T(8,128)(2,1)}, bf16[8,2,1024]{2,0,1:T(8,128)(2,1)S(1)}, u32[]{:S(2)}, u32[]{:S(2)}) collective-permute-start(bf16[8,2,1024]{2,0,1:T(8,128)(2,1)} %collective-permute-done.31), channel_id=1, source_target_pairs={{0,1},{1,2},{2,3},{3,4},{4,5},{5,6},{6,7},{7,8},{8,9},{9,10},{10,1... | collective-permute-start | bytes 98312 | tf_op jit(solution)/shard_map/ppermute | solution.py:140
  444.6 101.1 %collective-permute-start.36 = (bf16[8,2,1024]{2,0,1:T(8,128)(2,1)S(1)}, bf16[8,2,1024]{2,0,1:T(8,128)(2,1)S(1)}, u32[]{:S(2)}, u32[]{:S(2)}) collective-permute-start(bf16[8,2,1024]{2,0,1:T(8,128)(2,1)S(1)} %collective-permute-done.34), channel_id=1, source_target_pairs={{0,15},{1,0},{2,1},{3,2},{4,3},{5,4},{6,5},{7,6},{8,7},{9,8},{10,9... | collective-permute-start | bytes 98312 | tf_op jit(solution)/shard_map/ppermute | solution.py:146
  449.4 103.2 %collective-permute-start.37 = (bf16[8,2,1024]{2,0,1:T(8,128)(2,1)S(1)}, bf16[8,2,1024]{2,0,1:T(8,128)(2,1)}, u32[]{:S(2)}, u32[]{:S(2)}) collective-permute-start(bf16[8,2,1024]{2,0,1:T(8,128)(2,1)S(1)} %collective-permute-done.35), channel_id=1, source_target_pairs={{0,1},{1,2},{2,3},{3,4},{4,5},{5,6},{6,7},{7,8},{8,9},{9,10},{10,1... | collective-permute-start | bytes 98312 | tf_op jit(solution)/shard_map/ppermute | solution.py:140
  (44 other events, 692.6 us)
Sparse Core Ops, SparseCore 0:
  57.6 54.7 reduce-scatter.2
  351.2 54.5 reduce-scatter.4
